TPU v7x, 32 devices: a whole 2x2x4 slice. The times are simulated.
32 devices in a mesh: groups: 2 (over x), sph: 16 (over z, y, core).
Axes of the slice: x: 2, y: 2, z: 4, core: 2. Of those that a mesh axis runs over, the one named last changes fastest.
Arguments:
- positions: float32 [512, 3], P('sph'), may hold values from -8 to 8
- wave_vectors: float32 [256, 3], replicated, may hold values from -5 to 5
- pattern: float32 [2, 448, 256], replicated, may hold values from -6 to 6
- dir_index: int32 [64], P('groups'), parts along dimension 0, may hold values from 0 to 255
- mie: float32 [2, 448, 512], P(None, None, 'sph'), may hold values from -0.9 to 0.9
- trans_table: bfloat16 [8, 2, 448, 448], replicated, may hold values from -0.1875 to 0.1875
- pair_route: int32 [1024, 1], P('sph'), may hold values from 0 to 15; in each aligned block of 64 rows (0 to 63, 64 to 127, ...) at most 8 rows name the same one
- pair_source: int32 [1024], P('sph'), may hold values from 0 to 15
- pair_target: int32 [1024], P('sph'), may hold values from 0 to 15
- pair_class: int32 [1024], P('sph'), may hold values from 0 to 7
Outputs:
- scattered: bfloat16 [896, 32768], P(None, ('groups', 'sph')), parts along dimension 1
- extinction: float32 [64], P('groups'), parts along dimension 0
There are 2 independent parts, one for each index of `groups`. A program takes and returns all parts, laid end to end along the dimension named above; an argument that names none is the same for every part. Nothing has to cross between parts.
Inputs may be any that keep to these rules, and one draw needn't show every extreme that they name: `pair_route`: among the rows of one device no device is named by more than 8 pairs, and in every draw some device is named by exactly 8 of them.
All inputs are finite; a program needn't handle non-finite values.
Results may differ from a plain program's by a relative error of at most 0.0051.
Values may be sent and summed in bfloat16 or wider, within the bound.
A program may use at most 192 MiB of HBM per device.

v0:
```python
import jax
import jax.numpy as jnp
from jax import lax
from jax.sharding import PartitionSpec as P

BLOCK = 2


HIGHEST_PRECISION = lax.Precision.HIGHEST


def incident_field(positions, wave_vectors, pattern, dir_index):
    table_rows = wave_vectors.shape[0]
    select = (jnp.arange(table_rows, dtype=jnp.int32)[:, None] == dir_index[None, :]).astype(
        jnp.float32
    )
    directions = jnp.dot(select.T, wave_vectors, precision=HIGHEST_PRECISION)
    phases = (
        positions[:, 0:1] * directions[None, :, 0]
        + positions[:, 1:2] * directions[None, :, 1]
        + positions[:, 2:3] * directions[None, :, 2]
    )
    cosine = jnp.cos(phases)
    sine_part = jnp.sin(phases)
    chosen = jnp.einsum("cmt,td->cmd", pattern, select, precision=HIGHEST_PRECISION)
    inc_real = cosine[None] * chosen[0][:, None, :] - sine_part[None] * chosen[1][:, None, :]
    inc_imag = cosine[None] * chosen[1][:, None, :] + sine_part[None] * chosen[0][:, None, :]
    return (inc_real, inc_imag)


def translate(trans_table, classes, block_values):
    item_count = classes.shape[0]
    mode_count = trans_table.shape[2]
    grouped_classes = classes.reshape(item_count // 8, 8)
    grouped_values = block_values.reshape((item_count // 8, 8) + block_values.shape[1:])

    def one_group(group_items):
        picked, values = group_items
        tables = trans_table[picked]
        data_real = values[:, :mode_count]
        data_imag = values[:, mode_count:]
        part_real = jnp.einsum(
            "kij,kjc->kic", tables[:, 0], data_real, preferred_element_type=jnp.float32
        ) - jnp.einsum("kij,kjc->kic", tables[:, 1], data_imag, preferred_element_type=jnp.float32)
        part_imag = jnp.einsum(
            "kij,kjc->kic", tables[:, 1], data_real, preferred_element_type=jnp.float32
        ) + jnp.einsum("kij,kjc->kic", tables[:, 0], data_imag, preferred_element_type=jnp.float32)
        return jnp.concatenate([part_real, part_imag], 1).astype(jnp.bfloat16)

    return lax.map(one_group, (grouped_classes, grouped_values)).reshape(block_values.shape)


def shards(
    positions,
    wave_vectors,
    pattern,
    dir_index,
    mie,
    trans_table,
    pair_route,
    pair_source,
    pair_target,
    pair_class,
):
    mode_count = pattern.shape[1]
    spheres = positions.shape[0]
    directions = dir_index.shape[0]
    columns = BLOCK * directions
    block_count = spheres // BLOCK
    devices = lax.axis_size("sph")
    pair_count = pair_source.shape[0]
    capacity = max(2, 2 * pair_count // devices)
    slot_count = devices * capacity
    inc_real, inc_imag = incident_field(positions, wave_vectors, pattern, dir_index)
    mie_real = mie[0][:, :, None]
    mie_imag = mie[1][:, :, None]
    scat_real = mie_real * inc_real - mie_imag * inc_imag
    scat_imag = mie_real * inc_imag + mie_imag * inc_real
    coeffs = jnp.concatenate([scat_real, scat_imag], 0).astype(jnp.bfloat16)
    block_data = coeffs.reshape(2 * mode_count, block_count, columns).transpose(1, 0, 2)
    dest_device = pair_route[:, 0]
    by_device = (dest_device[:, None] == jnp.arange(devices, dtype=jnp.int32)[None, :]).astype(
        jnp.int32
    )
    before = jnp.cumsum(by_device, axis=0) - by_device
    rank_in = jnp.sum(before * by_device, axis=1)
    slot_of = dest_device * capacity + rank_in
    slot_match = (jnp.arange(slot_count, dtype=jnp.int32)[:, None] == slot_of[None, :]).astype(
        jnp.int32
    )
    filled = jnp.sum(slot_match, axis=1)
    slot_pair = jnp.sum(slot_match * jnp.arange(pair_count, dtype=jnp.int32)[None, :], axis=1)
    slot_target = jnp.where(filled > 0, pair_target[slot_pair], -1)
    keep_slot = filled.astype(jnp.bfloat16)[:, None, None]
    computed = translate(trans_table, pair_class, block_data[pair_source])
    outgoing = computed[slot_pair] * keep_slot
    outgoing = outgoing.reshape(devices, capacity, 2 * mode_count, columns)
    arrived = lax.all_to_all(outgoing, "sph", split_axis=0, concat_axis=0, tiled=True)
    targets = lax.all_to_all(
        slot_target.reshape(devices, capacity), "sph", split_axis=0, concat_axis=0, tiled=True
    ).reshape(slot_count)
    partial_value = arrived.reshape(slot_count, 2 * mode_count, columns)
    gather_matrix = (jnp.arange(block_count, dtype=jnp.int32)[:, None] == targets[None, :]).astype(
        jnp.bfloat16
    )
    summed = jnp.dot(
        gather_matrix,
        partial_value.reshape(slot_count, 2 * mode_count * columns),
        preferred_element_type=jnp.float32,
    )
    summed = (
        summed.reshape(block_count, 2 * mode_count, columns)
        .transpose(1, 0, 2)
        .reshape(2 * mode_count, spheres, directions)
    )
    total_real = inc_real + summed[:mode_count]
    total_imag = inc_imag + summed[mode_count:]
    out_real = mie_real * total_real - mie_imag * total_imag
    out_imag = mie_real * total_imag + mie_imag * total_real
    scattered = (
        jnp.concatenate([out_real, out_imag], 0)
        .reshape(2 * mode_count, spheres * directions)
        .astype(jnp.bfloat16)
    )
    local_ext = jnp.sum(inc_real * out_real + inc_imag * out_imag, axis=(0, 1))
    extinction = lax.psum(local_ext, "sph")
    return (scattered, extinction)


def solution(mesh):
    placed = (
        P("sph", None),
        P(),
        P(),
        P("groups"),
        P(None, None, "sph"),
        P(),
        P("sph", None),
        P("sph"),
        P("sph"),
        P("sph"),
    )
    return jax.shard_map(
        shards,
        mesh=mesh,
        in_specs=placed,
        out_specs=(P(None, ("groups", "sph")), P("groups")),
        check_vma=False,
    )
```

profile of v0, /device:TPU:0, one launch (start us, length us, event | category | flops | bytes accessed | tf_op | source)
XLA Modules:
  0.0 671.1 jit_solution(2450275542576880069)
XLA Ops:
  3.2 1.6 gather_fusion.1
  5.5 7.4 %all-to-all-start = ((s32[16,1,8]{2,1,0:T(1,128)}), s32[16,1,8]{2,1,0:T(1,128)S(1)}, u32[]{:S(2)}, u32[]{:S(2)}) async-start(s32[16,1,8]{2,1,0:T(1,128)} %bitcast.24), calls=%async_computation | async-start | bytes 16384 | tf_op jit(solution)/shard_map/all_to_all | solution.py:99
  16.3 1.2 convolution_bitcast_fusion
  21.9 4.3 gather_fusion.2
  26.3 134.5 %while.10 = (s32[]{:T(128)}, bf16[8,8,896,64]{2,3,1,0:T(8,128)(2,1)}, s32[8,8]{1,0:T(8,128)S(1)}, bf16[8,2,448,448]{3,2,1,0:T(8,128)(2,1)}, bf16[8,8,896,64]{2,3,1,0:T(8,128)(2,1)}, /*index=5*/s32[]{:T(128)}) while((s32[]{:T(128)}, bf16[8,8,896,64]{2,3,1,0:T(8,128)(2,1)}, s32[8,8]{1,0:T(8,128)S(1)}, bf16[8,2,448,448]{3,2,1,0:T(8,128)(2,1)}, ...), condition=%wide.region_5.6_spmd, body=%wide.region_4.5_spmd.sunk | while | flops 824837120 | bytes 63836904 | solution.py:50
  26.3 7.0 %gather_fusion = bf16[8,2,448,448]{3,2,1,0:T(8,128)(2,1)} fusion(bf16[8,2,448,448]{3,2,1,0:T(8,128)(2,1)} %get-tuple-element.133, s32[1024]{0:T(1024)S(1)} %pad_clamp_fusion.4), kind=kCustom, calls=%fused_computation.clone.1 | custom fusion | bytes 12845088 | tf_op jit(solution)/shard_map/while/body/eval_jaxpr/gather | solution.py:39
  33.3 1.4 dynamic-slice_bitcast_fusion.2
  34.7 3.5 fusion.68
  38.2 1.2 fusion.69
  41.8 1.3 maximum_dynamic-update-slice_fusion.2
  43.1 7.0 %gather_fusion = bf16[8,2,448,448]{3,2,1,0:T(8,128)(2,1)} fusion(bf16[8,2,448,448]{3,2,1,0:T(8,128)(2,1)} %get-tuple-element.133, s32[1024]{0:T(1024)S(1)} %pad_clamp_fusion.4), kind=kCustom, calls=%fused_computation.clone.1 | custom fusion | bytes 12845088 | tf_op jit(solution)/shard_map/while/body/eval_jaxpr/gather | solution.py:39
  50.1 1.4 dynamic-slice_bitcast_fusion.2
  51.5 3.5 fusion.68
  55.0 1.2 fusion.69
  56.2 1.2 fusion.66
  58.6 1.3 maximum_dynamic-update-slice_fusion.2
  59.9 7.0 %gather_fusion = bf16[8,2,448,448]{3,2,1,0:T(8,128)(2,1)} fusion(bf16[8,2,448,448]{3,2,1,0:T(8,128)(2,1)} %get-tuple-element.133, s32[1024]{0:T(1024)S(1)} %pad_clamp_fusion.4), kind=kCustom, calls=%fused_computation.clone.1 | custom fusion | bytes 12845088 | tf_op jit(solution)/shard_map/while/body/eval_jaxpr/gather | solution.py:39
  66.9 1.4 dynamic-slice_bitcast_fusion.2
  68.3 3.5 fusion.68
  71.8 1.2 fusion.69
  73.0 1.2 fusion.66
  75.4 1.3 maximum_dynamic-update-slice_fusion.2
  76.7 7.0 %gather_fusion = bf16[8,2,448,448]{3,2,1,0:T(8,128)(2,1)} fusion(bf16[8,2,448,448]{3,2,1,0:T(8,128)(2,1)} %get-tuple-element.133, s32[1024]{0:T(1024)S(1)} %pad_clamp_fusion.4), kind=kCustom, calls=%fused_computation.clone.1 | custom fusion | bytes 12845088 | tf_op jit(solution)/shard_map/while/body/eval_jaxpr/gather | solution.py:39
  83.7 1.4 dynamic-slice_bitcast_fusion.2
  85.1 3.5 fusion.68
  88.6 1.2 fusion.69
  89.8 1.2 fusion.66
  92.2 1.3 maximum_dynamic-update-slice_fusion.2
  93.5 7.0 %gather_fusion = bf16[8,2,448,448]{3,2,1,0:T(8,128)(2,1)} fusion(bf16[8,2,448,448]{3,2,1,0:T(8,128)(2,1)} %get-tuple-element.133, s32[1024]{0:T(1024)S(1)} %pad_clamp_fusion.4), kind=kCustom, calls=%fused_computation.clone.1 | custom fusion | bytes 12845088 | tf_op jit(solution)/shard_map/while/body/eval_jaxpr/gather | solution.py:39
  100.5 1.4 dynamic-slice_bitcast_fusion.2
  101.9 3.5 fusion.68
  105.4 1.2 fusion.69
  106.6 1.2 fusion.66
  109.0 1.3 maximum_dynamic-update-slice_fusion.2
  110.3 7.0 %gather_fusion = bf16[8,2,448,448]{3,2,1,0:T(8,128)(2,1)} fusion(bf16[8,2,448,448]{3,2,1,0:T(8,128)(2,1)} %get-tuple-element.133, s32[1024]{0:T(1024)S(1)} %pad_clamp_fusion.4), kind=kCustom, calls=%fused_computation.clone.1 | custom fusion | bytes 12845088 | tf_op jit(solution)/shard_map/while/body/eval_jaxpr/gather | solution.py:39
  117.3 1.4 dynamic-slice_bitcast_fusion.2
  118.7 3.5 fusion.68
  122.2 1.2 fusion.69
  123.4 1.2 fusion.66
  125.8 1.3 maximum_dynamic-update-slice_fusion.2
  127.1 7.0 %gather_fusion = bf16[8,2,448,448]{3,2,1,0:T(8,128)(2,1)} fusion(bf16[8,2,448,448]{3,2,1,0:T(8,128)(2,1)} %get-tuple-element.133, s32[1024]{0:T(1024)S(1)} %pad_clamp_fusion.4), kind=kCustom, calls=%fused_computation.clone.1 | custom fusion | bytes 12845088 | tf_op jit(solution)/shard_map/while/body/eval_jaxpr/gather | solution.py:39
  134.1 1.4 dynamic-slice_bitcast_fusion.2
  135.5 3.4 fusion.68
  139.0 1.2 fusion.69
  140.2 1.2 fusion.66
  142.6 1.3 maximum_dynamic-update-slice_fusion.2
  144.0 7.0 %gather_fusion = bf16[8,2,448,448]{3,2,1,0:T(8,128)(2,1)} fusion(bf16[8,2,448,448]{3,2,1,0:T(8,128)(2,1)} %get-tuple-element.133, s32[1024]{0:T(1024)S(1)} %pad_clamp_fusion.4), kind=kCustom, calls=%fused_computation.clone.1 | custom fusion | bytes 12845088 | tf_op jit(solution)/shard_map/while/body/eval_jaxpr/gather | solution.py:39
  151.0 1.4 dynamic-slice_bitcast_fusion.2
  152.4 3.5 fusion.68
  155.9 1.2 fusion.69
  157.1 1.2 fusion.66
  159.5 1.3 maximum_dynamic-update-slice_fusion.2
  160.7 12.2 %gather_fusion.3 = bf16[128,896,64]{1,2,0:T(8,128)(2,1)} fusion(bf16[64,896,64]{1,2,0:T(8,128)(2,1)} %bitcast.33, s32[1024]{0:T(1024)S(1)} %pad_clamp_fusion.2), kind=kCustom, calls=%fused_computation.3 | custom fusion | bytes 29360640 | tf_op jit(solution)/shard_map/gather | solution.py:96
  173.1 13.5 %broadcast_multiply_fusion = bf16[16,8,896,64]{2,3,1,0:T(8,128)(2,1)} fusion(bf16[16,8,896,64]{2,3,1,0:T(8,128)(2,1)} %bitcast.236, bf16[16,8]{1,0:T(8,128)(2,1)S(1)} %convert_element_type.32), kind=kLoop, calls=%fused_computation.29 | loop fusion | flops 7340032 | bytes 29360384 | tf_op jit(solution)/shard_map/mul | solution.py:96
  186.6 6.0 all-to-all-start.1
  194.7 258.1 %all-to-all-done.1 = bf16[16,8,896,64]{2,3,1,0:T(8,128)(2,1)} async-done(((bf16[16,8,896,64]{2,3,1,0:T(8,128)(2,1)}), bf16[16,8,896,64]{2,3,1,0:T(8,128)(2,1)}, u32[]{:S(2)}, u32[]{:S(2)}) %all-to-all-start.1) | async-done | bytes 14680096 | tf_op jit(solution)/shard_map/all_to_all | solution.py:98
  452.8 26.5 %copy.80 = bf16[16,8,896,64]{3,2,1,0:T(8,128)(2,1)} copy(bf16[16,8,896,64]{2,3,1,0:T(8,128)(2,1)} %all-to-all-done.1) | data formatting | bytes 29360128 | tf_op jit(solution)/shard_map/all_to_all | solution.py:98
  479.3 28.1 %reshape_reshape.3 = bf16[128,57344]{1,0:T(8,128)(2,1)} reshape(bf16[16,8,896,64]{3,2,1,0:T(8,128)(2,1)} %copy.80) | data formatting | bytes 29360128 | tf_op jit(solution)/shard_map/reshape;reshape | solution.py:108
  507.4 20.2 %copy.81 = bf16[57344,128]{1,0:T(8,128)(2,1)} copy(bf16[57344,128]{0,1:T(8,128)(2,1)} %bitcast.238) | data formatting | bytes 29360128 | tf_op jit(solution)/shard_map/dot_general | solution.py:106
  527.6 35.5 %fusion.34 = f32[896,16,64]{0,1,2:T(8,128)} fusion(bf16[896,64,128]{2,1,0:T(8,128)(2,1)} %bitcast.237, s32[128]{0:T(128)S(1)} %eq.64), kind=kOutput, calls=%fused_computation.61 | convolution fusion | flops 234883072 | bytes 18350592 | tf_op jit(solution)/shard_map/dot_general | solution.py:106
  563.1 9.9 %add_reduce_fusion = (f32[16,64]{0,1:T(8,128)S(1)}, f32[448,16,64]{0,1,2:T(8,128)S(1)}, f32[448,16,64]{0,1,2:T(8,128)S(1)}) fusion(f32[448,16,64]{0,2,1:T(8,128)S(1)} %bitcast.241, f32[448,16,64]{0,2,1:T(8,128)} %bitcast.247, f32[448,16,64]{0,2,1:T(8,128)S(1)} %bitcast.243, f32[448,16,64]{0,2,1:T(8,128)S(1)} %bitcast.245, f32[16,64]{0,1:T(8,128)S(1)} %copy.87, ...), kind=kLoop, calls=%fused_computation.60 | loop fusion | flops 8256512 | bytes 14692352 | tf_op jit(solution)/shard_map/reduce_sum | solution.py:125
  575.5 1.7 fusion.19
  577.8 2.4 copy.96
  580.4 90.4 %psum.7 = f32[32]{0:T(128)} all-reduce(f32[32]{0:T(128)S(1)} %reduce_sum.51), channel_id=1, replica_groups=mesh['groups'=2,'sph'=16] {'sph'}, use_global_device_ids=true, to_apply=%region_8.9 | all-reduce | flops 32 | bytes 256 | tf_op jit(solution)/shard_map/psum | solution.py:126
  (152 shorter events, 26.9 us)
Async XLA Ops:
  0.6 15.6 %copy-start = (f32[2,448,256]{2,1,0:T(8,128)S(1)}, f32[2,448,256]{2,1,0:T(8,128)}, u32[]{:S(2)}) copy-start(f32[2,448,256]{2,1,0:T(8,128)} %param.14) | copy-start | bytes 2752516
  0.6 16.9 %copy-start.20 = (s32[64]{0:T(128)S(1)}, s32[64]{0:T(128)}, u32[]{:S(2)}) copy-start(s32[64]{0:T(128)} %param.19) | copy-start | bytes 772
  0.7 16.9 %copy-start.19 = (s32[64]{0:T(128)S(1)}, s32[64]{0:T(128)}, u32[]{:S(2)}) copy-start(s32[64]{0:T(128)} %param.21) | copy-start | bytes 772
  0.7 17.0 %copy-start.18 = (f32[2,448,32]{1,2,0:T(8,128)S(1)}, f32[2,448,32]{1,2,0:T(8,128)}, u32[]{:S(2)}) copy-start(f32[2,448,32]{1,2,0:T(8,128)} %param.16) | copy-start | bytes 344068
  5.5 181.1 %all-to-all-start = ((s32[16,1,8]{2,1,0:T(1,128)}), s32[16,1,8]{2,1,0:T(1,128)S(1)}, u32[]{:S(2)}, u32[]{:S(2)}) async-start(s32[16,1,8]{2,1,0:T(1,128)} %bitcast.24), calls=%async_computation | async-start | bytes 16384 | tf_op jit(solution)/shard_map/all_to_all | solution.py:99
  17.7 0.6 copy-start.12
  17.7 0.6 copy-start.14
  17.7 0.6 copy-start.10
  17.7 0.9 copy-start.16
  18.0 1.3 copy-start.3
  18.3 1.7 copy-start.5
  18.6 2.5 copy-start.7
  18.9 2.5 copy-start.9
  33.3 4.9 copy-start.2
  50.1 4.9 copy-start.2
  66.9 4.9 copy-start.2
  83.7 4.9 copy-start.2
  100.5 4.9 copy-start.2
  117.3 4.9 copy-start.2
  134.1 4.9 copy-start.2
  151.0 4.9 copy-start.2
  186.6 266.2 %all-to-all-start.1 = ((bf16[16,8,896,64]{2,3,1,0:T(8,128)(2,1)}), bf16[16,8,896,64]{2,3,1,0:T(8,128)(2,1)}, u32[]{:S(2)}, u32[]{:S(2)}) async-start(bf16[16,8,896,64]{2,3,1,0:T(8,128)(2,1)} %broadcast_multiply_fusion), calls=%async_computation.1 | async-start | bytes 29360128 | tf_op jit(solution)/shard_map/all_to_all | solution.py:98
  527.6 35.5 %copy-start.4 = (f32[448,32,32]{0,2,1:T(8,128)S(1)}, f32[448,32,32]{0,2,1:T(8,128)}, u32[]{:S(2)}) copy-start(f32[448,32,32]{0,2,1:T(8,128)} %copy-done.3) | copy-start | bytes 5505028
  527.6 35.5 %copy-start.6 = (f32[448,32,32]{0,2,1:T(8,128)S(1)}, f32[448,32,32]{0,2,1:T(8,128)}, u32[]{:S(2)}) copy-start(f32[448,32,32]{0,2,1:T(8,128)} %copy-done.5) | copy-start | bytes 5505028
  527.6 35.5 %copy-start.8 = (f32[448,32,32]{0,2,1:T(8,128)S(1)}, f32[448,32,32]{0,2,1:T(8,128)}, u32[]{:S(2)}) copy-start(f32[448,32,32]{0,2,1:T(8,128)} %copy-done.7) | copy-start | bytes 5505028
  574.2 1.3 copy-start.11
  574.2 1.3 copy-start.13
  574.2 1.3 copy-start.15
  574.3 1.3 copy-start.17
  577.2 93.6 %copy-start.1 = (f32[2,448,256]{2,1,0:T(8,128)S(1)}, f32[2,448,256]{2,1,0:T(8,128)}, u32[]{:S(2)}) copy-start(f32[2,448,256]{2,1,0:T(8,128)} %param.14) | copy-start | bytes 2752516
where the time goes:
time: 683 us; the launch traced here: 671 us
  waiting for transfers between devices  258 us (38%)
  local copies, waits for them, and re-layouts  172 us (25%)
  matrix products  94.1 us (14%)
  blocking collectives  90.4 us (13%)
  other arithmetic  41 us (6%)
  starting transfers between devices  13.5 us (2%)
    all_to_all x1, waiting for transfers between devices, shards(): lax.all_to_all(outgoing, 'sph', split_axis=0, concat_axis=0, tiled=True)  258 us
    psum x1, blocking collectives, shards(): extinction = lax.psum(local_ext, 'sph')  90.4 us
    gather x8, local copies, waits for them, and re-layouts, one_group(): tables = trans_table[picked]  56.2 us
    dot_general x1, matrix products, shards(): jnp.dot(gather_matrix, partial_value.reshape(slot_count, 2 * mode_count *...  35.5 us
    another operation x1, local copies, waits for them, and re-layouts, shards(): partial_value.reshape(slot_count, 2 * mode_count * columns)  28.1 us
    dot_general x8, matrix products, one_group(): jnp.einsum('kij,kjc->kic', tables[:, 0], data_real, preferred_element_typ...  27.6 us
    all_to_all x1, local copies, waits for them, and re-layouts, shards(): lax.all_to_all(outgoing, 'sph', split_axis=0, concat_axis=0, tiled=True)  26.5 us
    dot_general x1, local copies, waits for them, and re-layouts, shards(): jnp.dot(gather_matrix, partial_value.reshape(slot_count, 2 * mode_count *...  20.2 us
  transfers between devices with their start and end apart: 2, of which 1 were waited for; matrix products, arithmetic and copies ran while one was open for 26% of the time, Pallas kernels for 0%

commit v1 on v0

v1 whole, which is shorter than its diff:
```python
import functools

import jax
import jax.numpy as jnp
from jax import lax
from jax.experimental import pallas as pl
from jax.experimental.pallas import tpu as pltpu
from jax.sharding import PartitionSpec as P

BLOCK = 2
LANES = 128
HIGHEST = lax.Precision.HIGHEST


def round_up(value, unit):
    return -(-value // unit) * unit


def field_kernel(
    dims, cells, sources, table, mie_rows, phase_rows, pat_rows, pat_tile, mie, cosine, sine,
    scattered, ext, head, chain, matrix, mixed, acc,
):
    modes, wide, dirs, blocks, classes, step_blocks = dims
    step = pl.program_id(0)
    columns = BLOCK * dirs
    slots = chain.shape[0]

    @pl.when(step == 0)
    def _():
        def clear(cell, carry):
            head[cell] = -1
            return carry

        lax.fori_loop(0, blocks * classes, clear, 0)

        def link(slot, carry):
            cell = cells[slot]

            @pl.when(cell >= 0)
            def _():
                chain[slot] = head[cell]
                head[cell] = slot

            return carry

        lax.fori_loop(0, slots, link, 0)
        for kind in range(classes):
            at = kind * 2 * wide
            if wide > modes:
                for part in range(2):
                    end = at + (part + 1) * wide
                    matrix[:, end - LANES : end] = jnp.zeros((2 * modes, LANES), matrix.dtype)
            real, imag = table[kind, 0], table[kind, 1]
            matrix[:modes, at : at + modes] = real
            matrix[:modes, at + wide : at + wide + modes] = -imag
            matrix[modes:, at : at + modes] = imag
            matrix[modes:, at + wide : at + wide + modes] = real

    def product(slot):
        block = sources[slot]
        spread = jnp.broadcast_to(phase_rows[pl.ds(block, 1), :], (2 * columns, 2 * columns)).T
        reals, imags = [], []
        for j in range(BLOCK):
            row = mie_rows[pl.ds(block * BLOCK + j, 1), :]
            mr, mi = row[:, :wide], row[:, wide:]
            c = jnp.concatenate([spread[j * dirs : (j + 1) * dirs]] * (wide // LANES), 1)
            s = jnp.concatenate([spread[columns + j * dirs : columns + (j + 1) * dirs]] * (wide // LANES), 1)
            reals.append(c * mr - s * mi)
            imags.append(c * mi + s * mr)
        return jnp.concatenate(reals, 0), jnp.concatenate(imags, 0)

    def build(index, carry):
        kind, local = index // step_blocks, index % step_blocks
        first = head[kind * blocks + step * step_blocks + local]
        rows = pl.ds(pl.multiple_of(local * columns, columns), columns)
        left = pl.ds(pl.multiple_of(kind * 2 * wide, 2 * wide), wide)
        right = pl.ds(pl.multiple_of(kind * 2 * wide + wide, wide), wide)

        @pl.when(first < 0)
        def _():
            zero = jnp.zeros((columns, wide), mixed.dtype)
            mixed[rows, left] = zero
            mixed[rows, right] = zero

        @pl.when(first >= 0)
        def _():
            yr, yi = product(first)
            acc[0] = yr
            acc[1] = yi

            def more(slot):
                yr, yi = product(slot)
                acc[0] += yr
                acc[1] += yi
                return chain[slot]

            lax.while_loop(lambda slot: slot >= 0, more, chain[first])
            yr, yi = acc[0], acc[1]
            pr, pi = pat_rows[0], pat_rows[1]
            mixed[rows, left] = (yr * pr - yi * pi).astype(mixed.dtype)
            mixed[rows, right] = (yr * pi + yi * pr).astype(mixed.dtype)

        return carry

    lax.fori_loop(0, classes * step_blocks, build, 0)
    interaction = lax.dot_general(
        matrix[...], mixed[...], (((1,), (1,)), ((), ())), preferred_element_type=jnp.float32
    )
    width = step_blocks * columns
    per_step = width // dirs
    spheres = mie.shape[1]
    picked = (
        lax.broadcasted_iota(jnp.int32, (spheres, width), 0)
        == step * per_step + lax.broadcasted_iota(jnp.int32, (spheres, width), 1) // dirs
    ).astype(jnp.float32)
    spread_mie = jnp.dot(mie[...], picked, precision=HIGHEST, preferred_element_type=jnp.float32)
    mr, mi = spread_mie[:modes], spread_mie[modes:]
    c, s = cosine[...], sine[...]
    pr = jnp.concatenate([pat_tile[0]] * (width // LANES), 1)
    pi = jnp.concatenate([pat_tile[1]] * (width // LANES), 1)
    inc_r = c * pr - s * pi
    inc_i = c * pi + s * pr
    total_r = inc_r + interaction[:modes]
    total_i = inc_i + interaction[modes:]
    out_r = mr * total_r - mi * total_i
    out_i = mr * total_i + mi * total_r
    scattered[:modes, :] = out_r.astype(scattered.dtype)
    scattered[modes:, :] = out_i.astype(scattered.dtype)
    ext[...] = jnp.sum(inc_r * out_r + inc_i * out_i, axis=0, keepdims=True)


def shards(
    positions, wave_vectors, pattern, dir_index, mie, trans_table, pair_route, pair_source,
    pair_target, pair_class,
):
    modes = pattern.shape[1]
    wide = round_up(modes, LANES)
    spheres = positions.shape[0]
    dirs = dir_index.shape[0]
    columns = BLOCK * dirs
    blocks = spheres // BLOCK
    classes = trans_table.shape[0]
    devices = lax.axis_size("sph")
    me = lax.axis_index("sph")
    pair_count = pair_source.shape[0]
    capacity = max(2, 2 * pair_count // devices)
    slots = devices * capacity
    tables = wave_vectors.shape[0]

    select = (jnp.arange(tables, dtype=jnp.int32)[:, None] == dir_index[None, :]).astype(jnp.float32)
    k = jnp.dot(select.T, wave_vectors, precision=HIGHEST)
    phases = (
        positions[:, 0:1] * k[None, :, 0]
        + positions[:, 1:2] * k[None, :, 1]
        + positions[:, 2:3] * k[None, :, 2]
    )
    cosine, sine = jnp.cos(phases), jnp.sin(phases)
    phase_rows = jnp.concatenate(
        [cosine.reshape(blocks, columns), sine.reshape(blocks, columns)], 1
    )
    dest = pair_route[:, 0]
    order = jnp.arange(pair_count, dtype=jnp.int32)
    rank = jnp.sum(
        ((dest[:, None] == dest[None, :]) & (order[None, :] < order[:, None])).astype(jnp.int32), 1
    )
    slot_of = dest * capacity + rank
    match = slot_of[:, None] == jnp.arange(slots, dtype=jnp.int32)[None, :]
    cell_of = pair_class * blocks + pair_target
    source_of = me * blocks + pair_source
    slot_cell = jnp.sum(jnp.where(match, cell_of[:, None] + 1, 0), 0) - 1
    slot_source = jnp.sum(jnp.where(match, source_of[:, None], 0), 0)
    lists = jnp.stack([slot_cell, slot_source]).astype(jnp.int32)
    mie_rows = jnp.pad(jnp.transpose(mie, (2, 0, 1)), ((0, 0), (0, 0), (0, wide - modes)))
    mie_rows = mie_rows.reshape(spheres, 2 * wide)

    all_mie = lax.all_gather(mie_rows, "sph", axis=0, tiled=True)
    all_phases = lax.all_gather(phase_rows, "sph", axis=0, tiled=True)
    all_lists = lax.all_gather(lists, "sph", axis=0)
    mine = lax.dynamic_slice_in_dim(all_lists, me * capacity, capacity, 2)
    cells = mine[:, 0].reshape(slots)
    sources = mine[:, 1].reshape(slots)

    select_tile = jnp.concatenate([select] * (LANES // dirs), 1)
    pat_tile = jnp.einsum("cmt,td->cmd", pattern, select_tile, precision=HIGHEST)
    pat_rows = jnp.einsum("td,cmt->cdm", select, pattern, precision=HIGHEST)
    pat_rows = jnp.pad(jnp.concatenate([pat_rows] * BLOCK, 1), ((0, 0), (0, 0), (0, wide - modes)))

    step_blocks = 2 * LANES // columns
    width = step_blocks * columns
    once = pl.Buffered(1)

    def whole(array):
        zeros = (0,) * array.ndim
        return pl.BlockSpec(array.shape, lambda i, *_: zeros, pipeline_mode=once)

    flat_mie = mie.reshape(2 * modes, spheres)
    operands = (trans_table, all_mie, all_phases, pat_rows, pat_tile, flat_mie)
    line = pl.BlockSpec((1, width), lambda i, *_: (0, i))
    depth = classes * 2 * wide
    scattered, ext = pl.pallas_call(
        functools.partial(field_kernel, (modes, wide, dirs, blocks, classes, step_blocks)),
        grid_spec=pltpu.PrefetchScalarGridSpec(
            num_scalar_prefetch=2,
            grid=(blocks // step_blocks,),
            in_specs=[whole(x) for x in operands] + [line, line],
            out_specs=[pl.BlockSpec((2 * modes, width), lambda i, *_: (0, i)), line],
            scratch_shapes=[
                pltpu.SMEM((blocks * classes,), jnp.int32),
                pltpu.SMEM((slots,), jnp.int32),
                pltpu.VMEM((2 * modes, depth), jnp.bfloat16),
                pltpu.VMEM((width, depth), jnp.bfloat16),
                pltpu.VMEM((2, columns, wide), jnp.float32),
            ],
        ),
        out_shape=[
            jax.ShapeDtypeStruct((2 * modes, spheres * dirs), jnp.bfloat16),
            jax.ShapeDtypeStruct((1, spheres * dirs), jnp.float32),
        ],
        compiler_params=pltpu.CompilerParams(
            dimension_semantics=("arbitrary",), vmem_limit_bytes=60 * 1024 * 1024
        ),
        name="field",
    )(cells, sources, *operands, cosine.reshape(1, spheres * dirs), sine.reshape(1, spheres * dirs))
    extinction = lax.psum(jnp.sum(ext.reshape(spheres, dirs), 0), "sph")
    return (scattered, extinction)


def solution(mesh):
    placed = (
        P("sph", None), P(), P(), P("groups"), P(None, None, "sph"), P(),
        P("sph", None), P("sph"), P("sph"), P("sph"),
    )
    return jax.shard_map(
        shards,
        mesh=mesh,
        in_specs=placed,
        out_specs=(P(None, ("groups", "sph")), P("groups")),
        check_vma=False,
    )
```

time: 683 us -> 144 us (0.21); the launches traced: 671 us -> 144 us
  waiting for transfers between devices: 258 us -> 0.02 us
  local copies, waits for them, and re-layouts: 172 us -> 8.87 us
  matrix products: 94.1 us -> 2.89 us
  other arithmetic: 41 us -> 4.8 us
  Pallas kernels: 0 us -> 35.4 us
  starting transfers between devices: 13.5 us -> 0.04 us
  between operations: 1.47 us -> 14.1 us
  blocking collectives: 90.4 us -> 78.1 us
    all_to_all x2 -> x0, waiting for transfers between devices: 258 us -> none  [the longest x1 258 us: shards(): lax.all_to_all(outgoing, 'sph', split_axis=0, concat_axis=0, tiled=True)]
    dot_general x35 -> x3, matrix products: 94.1 us -> 2.89 us  [the longest x1 1.45 us: shards(): jnp.einsum('cmt,td->cmd', pattern, select_tile, precision=HIGHEST)]
    gather x11 -> x0, local copies, waits for them, and re-layouts: 74.3 us -> none  [the longest x8 56.2 us: one_group(): tables = trans_table[picked]]
    psum x1, blocking collectives: 90.4 us -> 35.8 us  [shards(): extinction = lax.psum(jnp.sum(ext.reshape(spheres, dirs), 0), 'sph')]
    all_gather x0 -> x2, blocking collectives: none -> 42.4 us  [the longest x1 23.2 us: shards(): all_lists = lax.all_gather(lists, 'sph', axis=0)]
    pallas_call x0 -> x1, Pallas kernels: none -> 35.4 us  [shards(): pl.pallas_call(functools.partial(field_kernel, (modes, wide, dirs, blocks...]
    all_to_all x2 -> x0, local copies, waits for them, and re-layouts: 27 us -> none  [the longest x1 26.5 us: shards(): lax.all_to_all(outgoing, 'sph', split_axis=0, concat_axis=0, tiled=True)]
    another operation x1 -> x2, local copies, waits for them, and re-layouts: 28.1 us -> 1.26 us  [the longest x1 0.66 us: shards(): sources = mine[:, 1].reshape(slots)]
  transfers between devices with their start and end apart: 2 -> 1, of which waited for: 1 -> 0; matrix products, arithmetic and copies ran while one was open for 26% -> 9% of each run, Pallas kernels for 0% -> 0%
where the time goes in v1:
time: 144 us
  blocking collectives  78.1 us (54%)
  Pallas kernels  35.4 us (25%)
  between operations  14.1 us (10%)
  local copies, waits for them, and re-layouts  8.87 us (6%)
  other arithmetic  4.8 us (3%)
  matrix products  2.89 us (2%)
    psum x1, blocking collectives, shards(): extinction = lax.psum(jnp.sum(ext.reshape(spheres, dirs), 0), 'sph')  35.8 us
    pallas_call x1, Pallas kernels, shards(): pl.pallas_call(functools.partial(field_kernel, (modes, wide, dirs, blocks...  35.4 us
    all_gather x1, blocking collectives, shards(): all_lists = lax.all_gather(lists, 'sph', axis=0)  23.2 us
    all_gather x1, blocking collectives, shards(): all_phases = lax.all_gather(phase_rows, 'sph', axis=0, tiled=True)  19.2 us
    unnamed x7, local copies, waits for them, and re-layouts  3.63 us
  transfers between devices with their start and end apart: 1, of which 0 were waited for; matrix products, arithmetic and copies ran while one was open for 9% of the time, Pallas kernels for 0%

profile of v1, /device:TPU:0, one launch (start us, length us, event | category | flops | bytes accessed | tf_op | source)
XLA Modules:
  0.0 144.3 jit_solution(5785417067061816750)
XLA Ops:
  7.2 0.0 copy-start
  7.2 0.0 copy-start.1
  7.2 0.0 all-gather.4.cloned.1.call-start
  7.2 1.1 copy.26
  8.4 0.7 copy.27
  9.1 0.0 all-gather.4.cloned.1.call-update
  9.1 1.9 %copy.23 = f32[2,448,32]{2,1,0:T(8,128)} copy(f32[2,448,32]{1,2,0:T(8,128)} %param.14) | data formatting | bytes 229376 | tf_op args[4]
  10.9 0.8 slice_bitcast_fusion.5
  11.8 0.1 mul.160
  11.8 0.1 mul.161
  11.9 0.1 mul.162
  12.0 0.1 mul.168
  12.1 0.1 mul.169
  12.2 0.1 mul.170
  12.3 0.1 mul.176
  12.3 0.1 mul.177
  12.4 0.1 mul.178
  12.5 0.9 fusion.6
  13.4 0.1 mul.165
  13.5 0.1 mul.173
  13.6 0.1 mul.181
  13.7 0.1 fusion.14
  13.8 0.1 fusion.10
  13.9 0.7 cos.18.cosine
  14.6 0.7 sin.18.sine
  15.3 0.9 convert_reduce_fusion
  16.2 0.7 fusion.12
  16.9 0.7 add_add_fusion
  17.5 0.1 select_reduce_fusion.1
  17.7 23.2 %all-gather.1 = s32[16,2,128]{2,1,0:T(2,128)S(1)} all-gather(s32[1,2,128]{2,1,0:T(2,128)S(1)} %add_bitcast_fusion.2), channel_id=2, replica_groups=mesh['groups'=2,'sph'=16] {'sph'}, dimensions={0}, use_global_device_ids=true | all-gather | bytes 17408 | tf_op jit(solution)/shard_map/all_gather | solution.py:178
  40.8 0.1 dynamic-slice_reduce_fusion
  41.0 0.6 reshape_squeeze.6.cells
  41.6 0.7 reshape_squeeze.7.sources
  42.2 0.1 pad_maximum_fusion
  42.3 19.2 %all_gather.15.phase_rows = f32[256,128]{1,0:T(8,128)} all-gather(f32[16,128]{1,0:T(8,128)S(1)} %pad_maximum_fusion), channel_id=1, replica_groups=mesh['groups'=2,'sph'=16] {'sph'}, dimensions={0}, use_global_device_ids=true | all-gather | bytes 139264 | tf_op jit(solution)/shard_map/all_gather | solution.py:177
  61.5 0.0 copy-done
  61.5 0.0 copy-done.1
  61.5 0.6 convolution_bitcast_fusion.1
  62.1 0.7 select_maximum_fusion.pat_rows
  62.9 1.4 %convolution_bitcast_fusion.pat_tile = f32[2,448,128]{2,1,0:T(8,128)} fusion(f32[2,448,256]{2,1,0:T(8,128)S(1)} %copy-done, pred[256,32]{1,0:T(32,128)(4,1)S(1)} %iota_compare_fusion.1), kind=kOutput, calls=%fused_computation | convolution fusion | flops 352419840 | bytes 1384448 | tf_op jit(solution)/shard_map/cmt,td->cmd/dot_general | solution.py:184
  64.3 0.0 all-gather.4.cloned.1.call-done.mie_rows
  64.3 35.4 %field.1 = (bf16[896,1024]{1,0:T(8,128)(2,1)}, f32[1,1024]{1,0:T(1,128)}) custom-call(s32[128]{0:T(128)} %reshape_squeeze.6.cells, s32[128]{0:T(128)} %reshape_squeeze.7.sources, bf16[8,2,448,448]{3,2,1,0:T(8,128)(2,1)} %table.1, f32[512,1024]{1,0:T(8,128)} %all-gather.4.cloned.1.call-done.mie_rows, f32[256,128]{1,0:T(8,128)} %all_gather.15.phase_rows, ...), custom_call_target="tpu_custom_call" | custom-call | tf_op jit(solution)/shard_map/field/pallas_call | solution.py:200
  99.7 0.5 broadcast.89
  100.2 1.3 reduce.23
  101.5 0.1 reshape.179
  101.6 35.8 %psum.7 = f32[32]{0:T(128)} all-reduce(f32[32]{0:T(128)S(1)} %reduce_sum.42), channel_id=1, replica_groups=mesh['groups'=2,'sph'=16] {'sph'}, use_global_device_ids=true, to_apply=%region_4.5 | all-reduce | flops 32 | bytes 256 | tf_op jit(solution)/shard_map/psum | solution.py:224
  (10 shorter events, 0.2 us)
Async XLA Ops:
  7.2 54.3 %copy-start = (f32[2,448,256]{2,1,0:T(8,128)S(1)}, f32[2,448,256]{2,1,0:T(8,128)}, u32[]{:S(2)}) copy-start(f32[2,448,256]{2,1,0:T(8,128)} %param.12) | copy-start | bytes 2752516
  7.2 54.3 %copy-start.1 = (s32[32]{0:T(128)S(1)}, s32[32]{0:T(128)}, u32[]{:S(2)}) copy-start(s32[32]{0:T(128)} %param.13) | copy-start | bytes 388
  7.2 57.1 %all-gather.4.cloned.1.call-start = ((), (), s32[]{:S(2)}) async-start(), calls=%async_computation | async-start | bytes 2228224 | tf_op jit(solution)/shard_map/all_gather | solution.py:176
Sparse Core Ops, SparseCore 0:
  10.7 44.4 all-gather.3
